TPU v7x, 256 devices: a whole 4x4x8 slice. The times are simulated.
256 devices in a mesh: gx: 16 (over z, core), gy: 4 (over x), member: 4 (over y).
Axes of the slice: x: 4, y: 4, z: 8, core: 2. Of those that a mesh axis runs over, the one named last changes fastest.
Arguments:
- density: float32 [4, 64, 128, 256], P('member', 'gx', 'gy'), may hold values from 0.5 to 1.5
- velocity: float32 [4, 3, 64, 128, 256], P('member', None, 'gx', 'gy'), may hold values from -0.5 to 0.5
- pressure: float32 [4, 64, 128, 256], P('member', 'gx', 'gy'), may hold values from 0.5 to 1.5
- start_block: float32 [4, 128, 16], P('member'), may hold values from -6 to 6
- test_vectors: float32 [32, 64, 128], P('gx', 'gy'), may hold values from -48 to 48
Outputs:
- state_next: float32 [4, 5, 64, 128, 256], P('member', None, 'gx', 'gy')
- projected: float32 [32, 64, 128], P('gx', 'gy')
All inputs are finite; a program needn't handle non-finite values.
Results may differ from a plain program's by a relative error of at most 0.00013.
Values sent between devices are 32-bit elements; how exact they have to be, the bound alone decides.
A program may use at most 64 MiB of HBM per device.

v0:
```python
import jax
import jax.numpy as jnp
from jax import lax
from jax.sharding import PartitionSpec as P

HEAT_RATIO = 1.4
TIME_STEP = 0.08
PRECISE = lax.Precision.HIGHEST


def padded(block, sides, width):
    for axis, dim in sides:
        count = lax.axis_size(axis)
        forward = [(i, i + 1) for i in range(count - 1)]
        forward.append((count - 1, 0))
        backward = [(target, source) for source, target in forward]
        low = lax.ppermute(
            lax.slice_in_dim(block, block.shape[dim] - width, None, axis=dim), axis, forward
        )
        high = lax.ppermute(lax.slice_in_dim(block, 0, width, axis=dim), axis, backward)
        block = jnp.concatenate([low, block, high], axis=dim)
    return block


def cut(values, dimension, start_at, stop_at):
    return lax.slice_in_dim(values, start_at, stop_at, axis=dimension)


def conserved(density, velocity, pressure):
    momentum = density[None] * velocity
    energy = pressure / (HEAT_RATIO - 1.0) + 0.5 * density * jnp.sum(velocity * velocity, axis=0)
    return jnp.concatenate([density[None], momentum, energy[None]], axis=0)


def primitive(fields):
    velocity = fields[1:4] / fields[0]
    kinetic = 0.5 * jnp.sum(fields[1:4] * velocity, axis=0)
    pressure = (HEAT_RATIO - 1.0) * (fields[4] - kinetic)
    sound_speed = jnp.sqrt(HEAT_RATIO * pressure / fields[0])
    return (velocity, pressure, sound_speed)


def directed(fields, velocity, pressure, sound_speed, direction):
    normal = velocity[direction]
    components = [fields[1 + direction]]
    for component in range(3):
        moment_flux = fields[1 + component] * normal
        if component == direction:
            moment_flux = moment_flux + pressure
        components.append(moment_flux)
    components.append((fields[4] + pressure) * normal)
    return (jnp.stack(components), jnp.abs(normal) + sound_speed)


def tendency(fields):
    velocity, pressure, sound_speed = primitive(fields)
    summed = None
    for direction in range(3):
        fluxes, wave_speed = directed(fields, velocity, pressure, sound_speed, direction)
        if direction < 2:
            dimension = 1 + direction
            extent = fields.shape[dimension]
            left_flux = cut(fluxes, dimension, 0, extent - 1)
            right_flux = cut(fluxes, dimension, 1, extent)
            left_fields = cut(fields, dimension, 0, extent - 1)
            right_fields = cut(fields, dimension, 1, extent)
            bound_speed = jnp.maximum(
                cut(wave_speed, dimension - 1, 0, extent - 1),
                cut(wave_speed, dimension - 1, 1, extent),
            )
        else:
            left_flux = fluxes
            right_flux = jnp.roll(fluxes, -1, axis=3)
            left_fields = fields
            right_fields = jnp.roll(fields, -1, axis=3)
            bound_speed = jnp.maximum(wave_speed, jnp.roll(wave_speed, -1, axis=2))
        face_flux = 0.5 * (left_flux + right_flux) - 0.5 * bound_speed * (
            right_fields - left_fields
        )
        if direction < 2:
            change = cut(face_flux, dimension, 1, extent - 1) - cut(
                face_flux, dimension, 0, extent - 2
            )
            cross_dim = 2 - direction
            change = cut(change, cross_dim, 1, change.shape[cross_dim] - 1)
        else:
            change = face_flux - jnp.roll(face_flux, 1, axis=3)
            change = change[:, 1:-1, 1:-1]
        summed = change if summed is None else summed + change
    return -summed


def ghosted(fields):
    return padded(fields, (("gx", 1), ("gy", 2)), 1)


def shards(density, velocity, pressure, start_block, test_vectors):
    fields = conserved(density[0], velocity[0], pressure[0])
    section_one = fields + TIME_STEP * tendency(ghosted(fields))
    second = 0.5 * fields + 0.5 * (section_one + TIME_STEP * tendency(ghosted(section_one)))
    sampled = second[0, ::2, ::2, ::2]
    flattened = sampled.reshape(-1, sampled.shape[2])
    matrix = flattened - jnp.mean(flattened, axis=1, keepdims=True)
    sketch = jnp.dot(matrix, start_block[0], precision=PRECISE)
    folded = lax.psum(jnp.dot(matrix.T, sketch, precision=PRECISE), ("gx", "gy"))
    member_basis = jnp.dot(matrix, folded, precision=PRECISE)
    stacked = lax.all_gather(member_basis, "member", axis=1, tiled=True)
    vectors = test_vectors.reshape(-1, test_vectors.shape[2])
    gram_matrix, cross_terms = lax.psum(
        (
            jnp.dot(stacked.T, stacked, precision=PRECISE),
            jnp.dot(stacked.T, vectors, precision=PRECISE),
        ),
        ("gx", "gy"),
    )
    factor = jnp.linalg.cholesky(gram_matrix)
    halfway = lax.linalg.triangular_solve(factor, cross_terms, left_side=True, lower=True)
    coefficients = lax.linalg.triangular_solve(
        factor, halfway, left_side=True, lower=True, transpose_a=True
    )
    projected = jnp.dot(stacked, coefficients, precision=PRECISE).reshape(test_vectors.shape)
    return (second[None], projected)


def solution(mesh):
    return jax.shard_map(
        shards,
        mesh=mesh,
        in_specs=(
            P("member", "gx", "gy", None),
            P("member", None, "gx", "gy", None),
            P("member", "gx", "gy", None),
            P("member", None, None),
            P("gx", "gy", None),
        ),
        out_specs=(P("member", None, "gx", "gy", None), P("gx", "gy", None)),
        check_vma=False,
    )
```

profile of v0, /device:TPU:8, one launch (start us, length us, event | category | flops | bytes accessed | tf_op | source)
XLA Modules:
  0.0 563.6 jit_solution(3329118583548477129)
XLA Ops:
  0.7 1.1 bitcast_multiply_fusion.1
  1.8 1.0 fusion.45
  2.9 5.3 collective-permute-start.1
  8.2 3.0 collective-permute-done
  11.3 1.6 collective-permute-start.2
  12.8 1.7 collective-permute-start.3
  14.6 1.9 collective-permute-done.2
  16.4 0.3 collective-permute-done.3
  17.6 0.2 multiply_dynamic-update-slice_fusion.15
  18.0 0.4 slice.393
  18.4 0.4 slice.397
  18.8 0.2 fusion.16
  19.2 0.4 fusion.3
  19.7 0.2 fusion.57
  19.9 0.9 slice-done
  20.7 0.7 fusion.6
  21.5 0.2 slice.399
  21.7 0.6 fusion.28
  22.3 2.9 collective-permute-start.5
  25.3 3.0 collective-permute-done.4
  28.3 1.6 collective-permute-start.6
  29.9 1.7 collective-permute-start.7
  31.6 1.9 collective-permute-done.6
  33.5 0.3 collective-permute-done.7
  33.8 0.2 pad_maximum_fusion.1
  34.7 0.2 multiply_dynamic-update-slice_fusion.6
  35.0 0.4 slice.431
  35.5 0.4 slice.435
  35.9 0.2 fusion.13
  36.3 0.4 fusion.1
  36.7 0.2 fusion.56
  36.9 0.9 slice-done.1
  37.8 0.8 fusion.10
  38.5 0.2 slice.437
  38.8 0.6 fusion.23
  39.4 0.7 slice.363
  40.6 0.3 fusion.62
  40.9 250.3 %psum.21 = f32[128,16]{1,0:T(8,128)S(1)} all-reduce(f32[128,16]{1,0:T(8,128)S(1)} %fusion.62), channel_id=1, replica_groups=mesh['gx'=16,'gy'=4,'member'=4] {'gx','gy'}, use_global_device_ids=true, to_apply=%region_4.5 | all-reduce | flops 2048 | bytes 16384 | tf_op jit(solution)/shard_map/psum | solution.py:105
  291.2 0.2 fusion.63
  291.4 12.2 %all_gather.3 = f32[32,64]{0,1:T(8,128)S(1)} all-gather(f32[32,16]{0,1:T(8,128)S(1)} %fusion.63), channel_id=1, replica_groups=mesh['gx'=16,'gy'=4,'member'=4] {'member'}, dimensions={1}, use_global_device_ids=true | all-gather | bytes 10240 | tf_op jit(solution)/shard_map/all_gather | solution.py:107
  303.6 0.2 fusion.64
  304.0 246.2 %all-reduce = (f32[64,128]{1,0:T(8,128)S(1)}, f32[64,64]{0,1:T(8,128)S(1)}) all-reduce(f32[64,128]{1,0:T(8,128)S(1)} %fusion.65, f32[64,64]{0,1:T(8,128)S(1)} %fusion.64), channel_id=1, replica_groups=mesh['gx'=16,'gy'=4,'member'=4] {'gx','gy'}, use_global_device_ids=true, to_apply=%region_8.9 | all-reduce | flops 12288 | bytes 98304 | tf_op jit(solution)/shard_map/psum | solution.py:109
  550.2 5.8 %cholesky.16 = f32[64,64]{1,0:T(8,128)S(1)} custom-call(f32[64,64]{1,0:T(8,128)S(1)} %fusion.51), custom_call_target="Cholesky" | custom-call | tf_op jit(solution)/shard_map/jit(cholesky)/cholesky | solution.py:116
  556.1 0.6 compare_reduce_fusion
  556.7 0.7 fusion.46
  557.4 4.9 custom-call.8
  562.3 0.3 fusion.49
  562.7 0.8 fusion.66
  (67 shorter events, 3.4 us)
Async XLA Ops:
  0.6 303.2 %copy-start = (f32[2,16,128]{2,1,0:T(8,128)S(1)}, f32[2,16,128]{2,1,0:T(8,128)}, u32[]{:S(2)}) copy-start(f32[2,16,128]{2,1,0:T(8,128)} %param.9) | copy-start | bytes 49156
  0.6 2.1 copy-start.3
  2.9 8.3 %collective-permute-start = (f32[5,1,32,256]{3,2,1,0:T(8,128)S(1)}, f32[5,1,32,256]{3,2,1,0:T(8,128)S(1)}, u32[]{:S(2)}, u32[]{:S(2)}) collective-permute-start(f32[5,1,32,256]{3,2,1,0:T(8,128)S(1)} %get-tuple-element.62), channel_id=1, source_target_pairs={{0,16},{16,32},{32,48},{48,64},{64,80},{80,96},{96,112},{112,128},... | collective-permute-start | bytes 491528 | tf_op jit(solution)/shard_map/ppermute | solution.py:17
  2.9 8.3 %collective-permute-start.1 = (f32[5,1,32,256]{3,2,1,0:T(8,128)S(1)}, f32[5,1,32,256]{3,2,1,0:T(8,128)S(1)}, u32[]{:S(2)}, u32[]{:S(2)}) collective-permute-start(f32[5,1,32,256]{3,2,1,0:T(8,128)S(1)} %get-tuple-element.63), channel_id=1, source_target_pairs={{16,0},{32,16},{48,32},{64,48},{80,64},{96,80},{112,96},{128,112},... | collective-permute-start | bytes 491528 | tf_op jit(solution)/shard_map/ppermute | solution.py:20
  11.3 5.2 collective-permute-start.2
  12.8 3.9 collective-permute-start.3
  16.9 1.9 copy-start.1
  19.6 1.1 slice-start
  22.3 6.0 %collective-permute-start.4 = (f32[5,1,32,256]{3,2,1,0:T(8,128)S(1)}, f32[5,1,32,256]{3,2,1,0:T(8,128)S(1)}, u32[]{:S(2)}, u32[]{:S(2)}) collective-permute-start(f32[5,1,32,256]{3,2,1,0:T(8,128)S(1)} %get-tuple-element.60), channel_id=1, source_target_pairs={{0,16},{16,32},{32,48},{48,64},{64,80},{80,96},{96,112},{112,128},... | collective-permute-start | bytes 491528 | tf_op jit(solution)/shard_map/ppermute | solution.py:17
  22.3 5.9 %collective-permute-start.5 = (f32[5,1,32,256]{3,2,1,0:T(8,128)S(1)}, f32[5,1,32,256]{3,2,1,0:T(8,128)S(1)}, u32[]{:S(2)}, u32[]{:S(2)}) collective-permute-start(f32[5,1,32,256]{3,2,1,0:T(8,128)S(1)} %get-tuple-element.61), channel_id=1, source_target_pairs={{16,0},{32,16},{48,32},{64,48},{80,64},{96,80},{112,96},{128,112},... | collective-permute-start | bytes 491528 | tf_op jit(solution)/shard_map/ppermute | solution.py:20
  28.3 5.2 collective-permute-start.6
  29.9 3.9 collective-permute-start.7
  33.9 1.9 copy-start.2
  36.7 1.1 slice-start.1
  38.8 1.7 copy-start.5
  39.4 524.1 %copy-start.4 = (f32[5,4,32,256]{3,2,1,0:T(8,128)}, f32[5,4,32,256]{3,2,1,0:T(8,128)S(1)}, u32[]{:S(2)}) copy-start(f32[5,4,32,256]{3,2,1,0:T(8,128)S(1)} %fusion.23) | copy-start | bytes 1966084
where the time goes:
time: 564 us
  blocking collectives  509 us (90%)
  other arithmetic  20.6 us (4%)
  starting transfers between devices  14.9 us (3%)
  waiting for transfers between devices  10.3 us (2%)
  local copies, waits for them, and re-layouts  5.75 us (1%)
    psum x1, blocking collectives, shards(): lax.psum(jnp.dot(matrix.T, sketch, precision=PRECISE), ('gx', 'gy'))  250 us
    psum x1, blocking collectives, shards(): lax.psum((jnp.dot(stacked.T, stacked, precision=PRECISE), jnp.dot(stacked...  246 us
    all_gather x1, blocking collectives, shards(): stacked = lax.all_gather(member_basis, 'member', axis=1, tiled=True)  12.2 us
    ppermute x4, starting transfers between devices, padded(): lax.ppermute(lax.slice_in_dim(block, 0, width, axis=dim), axis, backward)  11.7 us
  transfers between devices with their start and end apart: 8, of which 6 were waited for; matrix products, arithmetic and copies ran while one was open for 0% of the time, Pallas kernels for 0%

commit v1 on v0

--- a/solution.py
+++ b/solution.py
@@ -102,7 +102,8 @@
     flattened = sampled.reshape(-1, sampled.shape[2])
     matrix = flattened - jnp.mean(flattened, axis=1, keepdims=True)
     sketch = jnp.dot(matrix, start_block[0], precision=PRECISE)
-    folded = lax.psum(jnp.dot(matrix.T, sketch, precision=PRECISE), ("gx", "gy"))
+    page = jnp.dot(matrix.T, sketch, precision=PRECISE)
+    folded = lax.all_gather(page, ("gx", "gy")).sum(axis=0)
     member_basis = jnp.dot(matrix, folded, precision=PRECISE)
     stacked = lax.all_gather(member_basis, "member", axis=1, tiled=True)
     vectors = test_vectors.reshape(-1, test_vectors.shape[2])

time: 564 us -> 387 us (0.69)
  blocking collectives: 509 us -> 332 us
    psum x1 -> x0, blocking collectives: 250 us -> none  [shards(): lax.psum(jnp.dot(matrix.T, sketch, precision=PRECISE), ('gx', 'gy'))]
    all_gather x0 -> x1, blocking collectives: none -> 72.8 us  [shards(): folded = lax.all_gather(page, ('gx', 'gy')).sum(axis=0)]
where the time goes in v1:
time: 387 us
  blocking collectives  332 us (86%)
  other arithmetic  20.7 us (5%)
  starting transfers between devices  14.9 us (4%)
  waiting for transfers between devices  10.3 us (3%)
  local copies, waits for them, and re-layouts  5.86 us (2%)
    psum x1, blocking collectives, shards(): lax.psum((jnp.dot(stacked.T, stacked, precision=PRECISE), jnp.dot(stacked...  247 us
    all_gather x1, blocking collectives, shards(): folded = lax.all_gather(page, ('gx', 'gy')).sum(axis=0)  72.8 us
    all_gather x1, blocking collectives, shards(): stacked = lax.all_gather(member_basis, 'member', axis=1, tiled=True)  12.2 us
    ppermute x4, starting transfers between devices, padded(): lax.ppermute(lax.slice_in_dim(block, 0, width, axis=dim), axis, backward)  11.7 us
    ppermute x4, waiting for transfers between devices, padded(): lax.ppermute(lax.slice_in_dim(block, block.shape[dim] - width, None, axis...  9.71 us
  transfers between devices with their start and end apart: 8, of which 6 were waited for; matrix products, arithmetic and copies ran while one was open for 0% of the time, Pallas kernels for 0%

profile of v1, /device:TPU:8, one launch (start us, length us, event | category | flops | bytes accessed | tf_op | source)
XLA Modules:
  0.0 386.9 jit_solution(15764909479835458316)
XLA Ops:
  0.7 1.1 bitcast_multiply_fusion.1
  1.8 1.0 fusion.45
  2.9 5.3 %collective-permute-start.1 = (f32[5,1,32,256]{3,2,1,0:T(8,128)S(1)}, f32[5,1,32,256]{3,2,1,0:T(8,128)S(1)}, u32[]{:S(2)}, u32[]{:S(2)}) collective-permute-start(f32[5,1,32,256]{3,2,1,0:T(8,128)S(1)} %get-tuple-element.63), channel_id=1, source_target_pairs={{16,0},{32,16},{48,32},{64,48},{80,64},{96,80},{112,96},{128,112},... | collective-permute-start | bytes 491528 | tf_op jit(solution)/shard_map/ppermute | solution.py:20
  8.2 3.0 collective-permute-done
  11.3 1.6 collective-permute-start.2
  12.8 1.7 collective-permute-start.3
  14.6 1.9 collective-permute-done.2
  16.4 0.3 collective-permute-done.3
  16.7 0.2 pad_maximum_fusion
  17.6 0.2 multiply_dynamic-update-slice_fusion.15
  18.0 0.4 slice.393
  18.4 0.4 slice.397
  18.8 0.2 fusion.16
  19.2 0.4 fusion.3
  19.7 0.2 fusion.57
  19.9 0.9 slice-done
  20.7 0.7 fusion.6
  21.5 0.2 slice.399
  21.7 0.6 fusion.28
  22.3 2.9 collective-permute-start.5
  25.3 3.0 collective-permute-done.4
  28.3 1.6 collective-permute-start.6
  29.9 1.7 collective-permute-start.7
  31.6 1.9 collective-permute-done.6
  33.5 0.3 collective-permute-done.7
  33.8 0.2 pad_maximum_fusion.1
  34.7 0.2 multiply_dynamic-update-slice_fusion.6
  35.0 0.4 slice.431
  35.5 0.4 slice.435
  35.9 0.2 fusion.13
  36.3 0.4 fusion.1
  36.7 0.2 fusion.56
  36.9 0.9 slice-done.1
  37.8 0.8 fusion.10
  38.5 0.2 slice.437
  38.8 0.6 fusion.23
  39.4 0.7 slice.363
  40.8 72.8 %all-gather = f32[8192,16]{0,1:T(8,128)S(1)} all-gather(f32[128,16]{0,1:T(8,128)S(1)} %fusion.62), channel_id=2, replica_groups=mesh['gx'=16,'gy'=4,'member'=4] {'gx','gy'}, dimensions={0}, use_global_device_ids=true | all-gather | bytes 532480 | tf_op jit(solution)/shard_map/all_gather | solution.py:106
  113.9 12.2 %all_gather.11 = f32[32,64]{0,1:T(8,128)S(1)} all-gather(f32[32,16]{0,1:T(8,128)S(1)} %fusion.63), channel_id=1, replica_groups=mesh['gx'=16,'gy'=4,'member'=4] {'member'}, dimensions={1}, use_global_device_ids=true | all-gather | bytes 10240 | tf_op jit(solution)/shard_map/all_gather | solution.py:108
  126.0 0.2 fusion.64
  126.4 247.1 %all-reduce = (f32[64,128]{1,0:T(8,128)S(1)}, f32[64,64]{0,1:T(8,128)S(1)}) all-reduce(f32[64,128]{1,0:T(8,128)S(1)} %fusion.65, f32[64,64]{0,1:T(8,128)S(1)} %fusion.64), channel_id=1, replica_groups=mesh['gx'=16,'gy'=4,'member'=4] {'gx','gy'}, use_global_device_ids=true, to_apply=%region_8.9 | all-reduce | flops 12288 | bytes 98304 | tf_op jit(solution)/shard_map/psum | solution.py:110
  373.5 5.8 %cholesky.16 = f32[64,64]{1,0:T(8,128)S(1)} custom-call(f32[64,64]{1,0:T(8,128)S(1)} %fusion.51), custom_call_target="Cholesky" | custom-call | tf_op jit(solution)/shard_map/jit(cholesky)/cholesky | solution.py:117
  379.4 0.6 compare_reduce_fusion
  380.1 0.7 fusion.46
  380.7 4.9 %custom-call.8 = f32[1,64,64]{1,2,0:T(8,128)S(1)} custom-call(f32[1,64,64]{2,1,0:T(8,128)S(1)} %fusion.46), custom_call_target="InvertDiagBlocksLowerTriangular" | custom-call | tf_op jit(solution)/shard_map/triangular_solve | solution.py:119
  385.6 0.3 fusion.49
  385.9 0.2 fusion.47
  386.1 0.8 fusion.66
  (69 shorter events, 3.5 us)
Async XLA Ops:
  0.6 125.6 %copy-start = (f32[2,16,128]{2,1,0:T(8,128)S(1)}, f32[2,16,128]{2,1,0:T(8,128)}, u32[]{:S(2)}) copy-start(f32[2,16,128]{2,1,0:T(8,128)} %param.9) | copy-start | bytes 49156
  0.6 2.1 copy-start.3
  2.9 8.3 %collective-permute-start = (f32[5,1,32,256]{3,2,1,0:T(8,128)S(1)}, f32[5,1,32,256]{3,2,1,0:T(8,128)S(1)}, u32[]{:S(2)}, u32[]{:S(2)}) collective-permute-start(f32[5,1,32,256]{3,2,1,0:T(8,128)S(1)} %get-tuple-element.62), channel_id=1, source_target_pairs={{0,16},{16,32},{32,48},{48,64},{64,80},{80,96},{96,112},{112,128},... | collective-permute-start | bytes 491528 | tf_op jit(solution)/shard_map/ppermute | solution.py:17
  2.9 8.3 %collective-permute-start.1 = (f32[5,1,32,256]{3,2,1,0:T(8,128)S(1)}, f32[5,1,32,256]{3,2,1,0:T(8,128)S(1)}, u32[]{:S(2)}, u32[]{:S(2)}) collective-permute-start(f32[5,1,32,256]{3,2,1,0:T(8,128)S(1)} %get-tuple-element.63), channel_id=1, source_target_pairs={{16,0},{32,16},{48,32},{64,48},{80,64},{96,80},{112,96},{128,112},... | collective-permute-start | bytes 491528 | tf_op jit(solution)/shard_map/ppermute | solution.py:20
  11.3 5.2 %collective-permute-start.2 = (f32[5,6,1,256]{3,2,1,0:T(1,128)S(1)}, f32[5,6,1,256]{3,2,1,0:T(1,128)S(1)}, u32[]{:S(2)}, u32[]{:S(2)}) collective-permute-start(f32[5,6,1,256]{3,2,1,0:T(1,128)S(1)} %get-tuple-element.58), channel_id=1, source_target_pairs={{0,4},{4,8},{8,12},{12,0},{1,5},{5,9},{9,13},{13,1},{2,6},{6,10},{... | collective-permute-start | bytes 92168 | tf_op jit(solution)/shard_map/ppermute | solution.py:17
  12.8 3.9 %collective-permute-start.3 = (f32[5,6,1,256]{3,2,1,0:T(1,128)S(1)}, f32[5,6,1,256]{3,2,1,0:T(1,128)S(1)}, u32[]{:S(2)}, u32[]{:S(2)}) collective-permute-start(f32[5,6,1,256]{3,2,1,0:T(1,128)S(1)} %get-tuple-element.59), channel_id=1, source_target_pairs={{4,0},{8,4},{12,8},{0,12},{5,1},{9,5},{13,9},{1,13},{6,2},{10,6},{... | collective-permute-start | bytes 92168 | tf_op jit(solution)/shard_map/ppermute | solution.py:20
  16.9 1.9 copy-start.1
  19.6 1.1 slice-start
  22.3 6.0 %collective-permute-start.4 = (f32[5,1,32,256]{3,2,1,0:T(8,128)S(1)}, f32[5,1,32,256]{3,2,1,0:T(8,128)S(1)}, u32[]{:S(2)}, u32[]{:S(2)}) collective-permute-start(f32[5,1,32,256]{3,2,1,0:T(8,128)S(1)} %get-tuple-element.60), channel_id=1, source_target_pairs={{0,16},{16,32},{32,48},{48,64},{64,80},{80,96},{96,112},{112,128},... | collective-permute-start | bytes 491528 | tf_op jit(solution)/shard_map/ppermute | solution.py:17
  22.3 5.9 %collective-permute-start.5 = (f32[5,1,32,256]{3,2,1,0:T(8,128)S(1)}, f32[5,1,32,256]{3,2,1,0:T(8,128)S(1)}, u32[]{:S(2)}, u32[]{:S(2)}) collective-permute-start(f32[5,1,32,256]{3,2,1,0:T(8,128)S(1)} %get-tuple-element.61), channel_id=1, source_target_pairs={{16,0},{32,16},{48,32},{64,48},{80,64},{96,80},{112,96},{128,112},... | collective-permute-start | bytes 491528 | tf_op jit(solution)/shard_map/ppermute | solution.py:20
  28.3 5.2 %collective-permute-start.6 = (f32[5,6,1,256]{3,2,1,0:T(1,128)S(1)}, f32[5,6,1,256]{3,2,1,0:T(1,128)S(1)}, u32[]{:S(2)}, u32[]{:S(2)}) collective-permute-start(f32[5,6,1,256]{3,2,1,0:T(1,128)S(1)} %get-tuple-element.54), channel_id=1, source_target_pairs={{0,4},{4,8},{8,12},{12,0},{1,5},{5,9},{9,13},{13,1},{2,6},{6,10},{... | collective-permute-start | bytes 92168 | tf_op jit(solution)/shard_map/ppermute | solution.py:17
  29.9 3.9 %collective-permute-start.7 = (f32[5,6,1,256]{3,2,1,0:T(1,128)S(1)}, f32[5,6,1,256]{3,2,1,0:T(1,128)S(1)}, u32[]{:S(2)}, u32[]{:S(2)}) collective-permute-start(f32[5,6,1,256]{3,2,1,0:T(1,128)S(1)} %get-tuple-element.55), channel_id=1, source_target_pairs={{4,0},{8,4},{12,8},{0,12},{5,1},{9,5},{13,9},{1,13},{6,2},{10,6},{... | collective-permute-start | bytes 92168 | tf_op jit(solution)/shard_map/ppermute | solution.py:20
  33.9 1.9 copy-start.2
  36.7 1.1 slice-start.1
  38.8 1.7 copy-start.5
  39.4 86.8 %copy-start.4 = (f32[5,4,32,256]{3,2,1,0:T(8,128)}, f32[5,4,32,256]{3,2,1,0:T(8,128)S(1)}, u32[]{:S(2)}) copy-start(f32[5,4,32,256]{3,2,1,0:T(8,128)S(1)} %fusion.23) | copy-start | bytes 1966084
